TPU v7x, 32 devices: a whole 2x2x4 slice. The times are simulated.
32 devices in a mesh: row: 4 (over z), col: 8 (over y, x, core).
Axes of the slice: x: 2, y: 2, z: 4, core: 2. Of those that a mesh axis runs over, the one named last changes fastest.
Arguments:
- level_set: float32 [384, 384, 384], P('col', 'row'), may hold values from -7 to 7
- image: float32 [384, 384, 384], P('col', 'row'), may hold values from -6 to 6
Outputs:
- updated_level: float32 [384, 384, 384], P('col', 'row')
All inputs are finite; a program needn't handle non-finite values.
Results may differ from a plain program's by a relative error of at most 0.00021.
Values sent between devices are 32-bit elements; how exact they have to be, the bound alone decides.
No kernel may reach another device: no remote copies, remote signals or barrier semaphores. Data moves between devices by JAX's collectives and lax.ppermute only.
A program may use at most 192 MiB of HBM per device.

v0:
```python
import jax
import jax.numpy as jnp
from jax import lax
from jax.sharding import PartitionSpec as P

RADIUS = 6


sigma_cells = 8.0
dt_step = 0.5
nu_diff = 0.1
eps_fit = 0.05


def extended(value, sides, width):
    for axis, dim in sides:
        devices, length = (lax.axis_size(axis), value.shape[dim])
        up = [(i, (i + 1) % devices) for i in range(devices)]
        down = [(j, i) for i, j in up]
        last = lax.slice_in_dim(value, length - width, length, axis=dim)
        first = lax.slice_in_dim(value, 0, width, axis=dim)
        before = lax.ppermute(last, axis, up)
        after = lax.ppermute(first, axis, down)
        value = jnp.concatenate([before, value, after], axis=dim)
    return value


def tap_weight(offset):
    tap_offsets = lax.iota(jnp.int32, 2 * RADIUS + 1) - RADIUS
    tap_float = tap_offsets.astype(jnp.float32)
    total_weight = jnp.sum(jnp.exp(-tap_float * tap_float / (2.0 * sigma_cells * sigma_cells)))
    off_float = offset.astype(jnp.float32)
    inside = jnp.abs(offset) <= RADIUS
    weights = jnp.where(
        inside, jnp.exp(-off_float * off_float / (2.0 * sigma_cells * sigma_cells)), 0.0
    )
    return weights / total_weight


def gauss_table(length):
    indices = lax.iota(jnp.int32, length)
    distance = jnp.abs(indices[:, None] - indices[None, :])
    distance = jnp.minimum(distance, length - distance)
    return tap_weight(distance)


def band_table(count):
    padded_index = lax.iota(jnp.int32, count + 2 * RADIUS)
    output_index = lax.iota(jnp.int32, count)
    return tap_weight(padded_index[:, None] - RADIUS - output_index[None, :])


def fit_coeffs(smoothed):
    first, second, third, fourth = (smoothed[0], smoothed[1], smoothed[2], smoothed[3])
    inside_mean = first / (second + eps_fit)
    outside_mean = (third - first) / (1.0 - second + eps_fit)
    spread = fourth - third * third + eps_fit
    slope_term = 2.0 * (inside_mean - outside_mean) / spread
    offset = (outside_mean * outside_mean - inside_mean * inside_mean) / spread
    return jnp.stack([slope_term, offset])


def body(level_set, image):
    highest = lax.Precision.HIGHEST
    z_local, y_local, length = level_set.shape
    kernel_table = gauss_table(length)
    heaviside = 0.5 + jnp.arctan(level_set) / jnp.pi
    fields = jnp.stack([heaviside * image, heaviside, image, image * image])
    along_x = jnp.einsum("fzyx,xw->fzyw", fields, kernel_table, precision=highest)
    padded_y = extended(along_x, (("row", 2),), RADIUS)
    along_y = jnp.einsum("fzpx,pi->fzix", padded_y, band_table(y_local), precision=highest)
    padded_z = extended(along_y, (("col", 1),), RADIUS)
    smoothed = jnp.einsum("fpyx,pi->fiyx", padded_z, band_table(z_local), precision=highest)
    local_coeffs = fit_coeffs(smoothed)
    forcing = image * local_coeffs[0] + local_coeffs[1]
    padded = extended(level_set, (("row", 1), ("col", 0)), 1)
    laplace = (
        padded[2:, 1:-1, :]
        + padded[:-2, 1:-1, :]
        + padded[1:-1, 2:, :]
        + padded[1:-1, :-2, :]
        + jnp.roll(level_set, 1, 2)
        + jnp.roll(level_set, -1, 2)
        - 6.0 * level_set
    )
    dirac_weight = 1.0 / (jnp.pi * (1.0 + level_set * level_set))
    return level_set + dt_step * (nu_diff * laplace + dirac_weight * forcing)


def solution(mesh):
    return jax.shard_map(
        body,
        mesh=mesh,
        in_specs=(P("col", "row", None), P("col", "row", None)),
        out_specs=P("col", "row", None),
        check_vma=False,
    )
```

profile of v0, /device:TPU:0, one launch (start us, length us, event | category | flops | bytes accessed | tf_op | source)
XLA Modules:
  0.0 418.9 jit_solution(12528538565307529535)
XLA Ops:
  0.0 0.6 fusion.78
  0.6 0.9 fusion.102
  1.6 16.4 %multiply_bitcast_fusion.1 = (f32[1,48,96,384]{3,2,1,0:T(8,128)}, f32[1,48,96,384]{3,2,1,0:T(8,128)}, f32[1,48,96,384]{3,2,1,0:T(8,128)}) fusion(f32[48,96,384]{2,1,0:T(8,128)} %param.3, f32[48,96,384]{2,1,0:T(8,128)} %param.2), kind=kLoop, calls=%fused_computation.43 | loop fusion | flops 7077888 | bytes 35389440 | tf_op jit(solution)/shard_map/stack | solution.py:68
  17.9 59.5 %fusion.8 = f32[4,48,96,384]{3,2,1,0:T(8,128)S(1)} fusion(f32[1,48,96,384]{3,2,1,0:T(8,128)} %get-tuple-element.13, f32[1,48,96,384]{3,2,1,0:T(8,128)} %bitcast.45, f32[1,48,96,384]{3,2,1,0:T(8,128)} %get-tuple-element.12, f32[1,48,96,384]{3,2,1,0:T(8,128)} %get-tuple-element.11, f32[384,384,1,1]{1,0,3,2:T(8,128)S(1)} %fusion.102), kind=kOutput, calls=%fused_computation.9 | convolution fusion | flops 32636141568 | bytes 57212928 | tf_op jit(solution)/shard_map/fzyx,xw->fzyw/dot_general | solution.py:69
  77.4 0.3 fusion.92
  77.7 0.3 copy.5
  78.1 3.1 collective-permute-start.4
  81.2 0.3 copy.6
  81.5 2.1 collective-permute-start.5
  83.6 39.1 %collective-permute-done.4 = f32[4,48,6,384]{3,1,2,0:T(8,128)S(1)} collective-permute-done((f32[4,48,6,384]{3,1,2,0:T(8,128)S(1)}, f32[4,48,6,384]{3,1,2,0:T(8,128)S(1)}, u32[]{:S(2)}, u32[]{:S(2)}) %collective-permute-start.4) | collective-permute-done | bytes 1769504 | tf_op jit(solution)/shard_map/ppermute | solution.py:22
  122.7 0.6 copy.7
  123.3 36.2 %collective-permute-done.5 = f32[4,48,6,384]{3,1,2,0:T(8,128)S(1)} collective-permute-done((f32[4,48,6,384]{3,1,2,0:T(8,128)S(1)}, f32[4,48,6,384]{3,1,2,0:T(8,128)S(1)}, u32[]{:S(2)}, u32[]{:S(2)}) %collective-permute-start.5) | collective-permute-done | bytes 1769504 | tf_op jit(solution)/shard_map/ppermute | solution.py:23
  159.5 0.6 copy.8
  160.1 0.0 slice-start.1
  160.2 35.3 %fusion.16 = f32[4,48,96,384]{3,2,1,0:T(8,128)} fusion(f32[4,48,6,384]{3,2,1,0:T(8,128)S(1)} %copy.8, f32[4,48,96,384]{3,2,1,0:T(8,128)} %copy-done, f32[4,48,6,384]{3,2,1,0:T(8,128)S(1)} %copy.7, f32[]{:T(128)} %fusion.78, s32[108]{0:T(128)S(1)} %iota_add_fusion), kind=kOutput, calls=%fused_computation.18 | convolution fusion | flops 9188961280 | bytes 60162484 | tf_op jit(solution)/shard_map/fzpx,pi->fzix/dot_general | solution.py:71
  195.5 5.5 %fusion.91 = (f32[4,6,96,384]{3,2,1,0:T(8,128)}, f32[4,6,96,384]{3,2,1,0:T(8,128)S(1)}) fusion(f32[4,48,96,384]{3,2,1,0:T(8,128)} %fusion.16), kind=kLoop, calls=%fused_computation.115 | loop fusion | bytes 14155776 | tf_op jit(solution)/shard_map/slice | solution.py:20
  201.0 0.0 collective-permute-start.6
  201.0 2.6 collective-permute-start.7
  203.7 0.8 fusion.95
  204.4 0.8 collective-permute-start
  205.2 3.1 collective-permute-start.1
  208.3 3.0 fusion.94
  211.3 12.0 %fusion.93 = (f32[48,96,383]{2,1,0:T(8,128)}, f32[48,96,383]{2,1,0:T(8,128)}) fusion(f32[48,96,384]{2,1,0:T(8,128)} %param.2), kind=kLoop, calls=%fused_computation.117 | loop fusion | bytes 28237824 | tf_op jit(solution)/shard_map/jit(_roll_static)/slice | solution.py:83
  223.3 0.0 collective-permute-done
  223.3 1.7 pad_maximum_fusion.11
  225.1 0.5 collective-permute-start.3
  225.6 53.8 %collective-permute-done.6 = f32[4,6,96,384]{3,2,1,0:T(8,128)} collective-permute-done((f32[4,6,96,384]{3,2,1,0:T(8,128)}, f32[4,6,96,384]{3,2,1,0:T(8,128)}, u32[]{:S(2)}, u32[]{:S(2)}) %collective-permute-start.6) | collective-permute-done | bytes 3538976 | tf_op jit(solution)/shard_map/ppermute | solution.py:22
  279.4 1.2 collective-permute-done.7
  280.6 24.2 %pad_maximum_fusion = f32[4,60,96,384]{3,2,1,0:T(8,128)} fusion(f32[4,6,96,384]{3,2,1,0:T(8,128)} %collective-permute-done.7, f32[4,48,96,384]{3,2,1,0:T(8,128)} %fusion.16, f32[4,6,96,384]{3,2,1,0:T(8,128)} %collective-permute-done.6), kind=kLoop, calls=%fused_computation.2 | loop fusion | flops 17694720 | bytes 70778880 | tf_op jit(solution)/shard_map/concatenate | solution.py:24
  304.8 58.4 %fusion = f32[48,4,96,384]{3,0,2,1:T(8,128)S(1)} fusion(f32[4,60,96,384]{3,2,1,0:T(8,128)} %pad_maximum_fusion, f32[]{:T(128)} %fusion.78, s32[60]{0:T(128)S(1)} %iota_add_fusion.1), kind=kOutput, calls=%fused_computation | convolution fusion | flops 5096105472 | bytes 63701236 | tf_op jit(solution)/shard_map/fpyx,pi->fiyx/dot_general | solution.py:73
  363.2 16.7 %copy.17 = f32[48,4,96,384]{3,2,0,1:T(8,128)} copy(f32[48,4,96,384]{3,0,2,1:T(8,128)S(1)} %fusion) | data formatting | bytes 56623104 | tf_op jit(solution)/shard_map/fpyx,pi->fiyx/dot_general | solution.py:73
  379.9 38.8 %fusion.27 = f32[48,96,384]{2,1,0:T(8,128)} fusion(f32[48,96,384]{2,1,0:T(8,128)} %param.2, f32[48,1,384]{2,1,0:T(1,128)} %collective-permute-done, f32[48,1,384]{2,1,0:T(1,128)} %collective-permute-done.1, f32[1,98,384]{2,1,0:T(8,128)} %collective-permute-done.3, f32[1,98,384]{2,1,0:T(8,128)} %collective-permute-done.2, ...), kind=kLoop, calls=%fused_computation.29 | loop fusion | flops 76087296 | bytes 64149504 | tf_op jit(solution)/shard_map/add | solution.py:87
  (12 shorter events, 0.0 us)
Async XLA Ops:
  77.4 45.9 %copy-start = (f32[4,48,96,384]{3,2,1,0:T(8,128)}, f32[4,48,96,384]{3,2,1,0:T(8,128)S(1)}, u32[]{:S(2)}) copy-start(f32[4,48,96,384]{3,2,1,0:T(8,128)S(1)} %fusion.8) | copy-start | bytes 84934656
  78.1 44.6 %collective-permute-start.4 = (f32[4,48,6,384]{3,1,2,0:T(8,128)S(1)}, f32[4,48,6,384]{3,1,2,0:T(8,128)S(1)}, u32[]{:S(2)}, u32[]{:S(2)}) collective-permute-start(f32[4,48,6,384]{3,1,2,0:T(8,128)S(1)} %copy.5), channel_id=1, source_target_pairs={{0,8},{8,16},{16,24},{24,0},{1,9},{9,17},{17,25},{25,1},{2,10},{10... | collective-permute-start | bytes 5308424 | tf_op jit(solution)/shard_map/ppermute | solution.py:22
  81.5 78.0 %collective-permute-start.5 = (f32[4,48,6,384]{3,1,2,0:T(8,128)S(1)}, f32[4,48,6,384]{3,1,2,0:T(8,128)S(1)}, u32[]{:S(2)}, u32[]{:S(2)}) collective-permute-start(f32[4,48,6,384]{3,1,2,0:T(8,128)S(1)} %copy.6), channel_id=1, source_target_pairs={{8,0},{16,8},{24,16},{0,24},{9,1},{17,9},{25,17},{1,25},{10,2},{18... | collective-permute-start | bytes 5308424 | tf_op jit(solution)/shard_map/ppermute | solution.py:23
  159.5 44.1 %slice-start = ((s8[7077888]{0:T(1024)(128)(4,1)}), s8[4194304]{0:T(1024)(128)(4,1)S(1)}, s32[]{:S(2)}) async-start(s8[7077888]{0:T(1024)(128)(4,1)} %bitcast.42), calls=%async_computation | async-start | bytes 8388608
  160.1 43.5 %slice-start.1 = ((s8[7077888]{0:T(1024)(128)(4,1)}), s8[2883584]{0:T(1024)(128)(4,1)S(1)}, s32[]{:S(2)}) async-start(s8[7077888]{0:T(1024)(128)(4,1)} %bitcast.42), calls=%async_computation.1 | async-start | bytes 5767168
  201.0 78.4 %collective-permute-start.6 = (f32[4,6,96,384]{3,2,1,0:T(8,128)}, f32[4,6,96,384]{3,2,1,0:T(8,128)}, u32[]{:S(2)}, u32[]{:S(2)}) collective-permute-start(f32[4,6,96,384]{3,2,1,0:T(8,128)} %get-tuple-element.5), channel_id=1, source_target_pairs={{0,1},{1,2},{2,3},{3,4},{4,5},{5,6},{6,7},{7,0},{8,9},{9,10},{10,1... | collective-permute-start | bytes 10616840 | tf_op jit(solution)/shard_map/ppermute | solution.py:22
  201.0 79.6 %collective-permute-start.7 = (f32[4,6,96,384]{3,2,1,0:T(8,128)S(1)}, f32[4,6,96,384]{3,2,1,0:T(8,128)}, u32[]{:S(2)}, u32[]{:S(2)}) collective-permute-start(f32[4,6,96,384]{3,2,1,0:T(8,128)S(1)} %get-tuple-element.6), channel_id=1, source_target_pairs={{1,0},{2,1},{3,2},{4,3},{5,4},{6,5},{7,6},{0,7},{9,8},{10,9},{11,1... | collective-permute-start | bytes 10616840 | tf_op jit(solution)/shard_map/ppermute | solution.py:23
  204.4 18.9 %collective-permute-start = (f32[48,1,384]{2,1,0:T(1,128)}, f32[48,1,384]{2,1,0:T(1,128)}, u32[]{:S(2)}, u32[]{:S(2)}) collective-permute-start(f32[48,1,384]{2,1,0:T(1,128)} %get-tuple-element.19), channel_id=1, source_target_pairs={{0,8},{8,16},{16,24},{24,0},{1,9},{9,17},{17,25},{25,1},{2,10},{10... | collective-permute-start | bytes 221192 | tf_op jit(solution)/shard_map/ppermute | solution.py:22
  205.2 18.1 %collective-permute-start.1 = (f32[48,1,384]{2,1,0:T(1,128)}, f32[48,1,384]{2,1,0:T(1,128)}, u32[]{:S(2)}, u32[]{:S(2)}) collective-permute-start(f32[48,1,384]{2,1,0:T(1,128)} %get-tuple-element.18), channel_id=1, source_target_pairs={{8,0},{16,8},{24,16},{0,24},{9,1},{17,9},{25,17},{1,25},{10,2},{18... | collective-permute-start | bytes 221192 | tf_op jit(solution)/shard_map/ppermute | solution.py:23
  225.1 154.8 %collective-permute-start.2 = (f32[1,98,384]{2,1,0:T(8,128)}, f32[1,98,384]{2,1,0:T(8,128)}, u32[]{:S(2)}, u32[]{:S(2)}) collective-permute-start(f32[1,98,384]{2,1,0:T(8,128)} %get-tuple-element.9), channel_id=1, source_target_pairs={{1,0},{2,1},{3,2},{4,3},{5,4},{6,5},{7,6},{0,7},{9,8},{10,9},{11,1... | collective-permute-start | bytes 451592 | tf_op jit(solution)/shard_map/ppermute | solution.py:23
  225.1 154.8 %collective-permute-start.3 = (f32[1,98,384]{2,1,0:T(8,128)}, f32[1,98,384]{2,1,0:T(8,128)}, u32[]{:S(2)}, u32[]{:S(2)}) collective-permute-start(f32[1,98,384]{2,1,0:T(8,128)} %get-tuple-element.10), channel_id=1, source_target_pairs={{0,1},{1,2},{2,3},{3,4},{4,5},{5,6},{6,7},{7,0},{8,9},{9,10},{10,1... | collective-permute-start | bytes 451592 | tf_op jit(solution)/shard_map/ppermute | solution.py:22
where the time goes:
time: 424 us; the launch traced here: 419 us
  matrix products  153 us (36%)
  waiting for transfers between devices  130 us (31%)
  other arithmetic  82.7 us (20%)
  local copies, waits for them, and re-layouts  40.2 us (9%)
  starting transfers between devices  12.2 us (3%)
    ppermute x4, waiting for transfers between devices, extended(): before = lax.ppermute(last, axis, up)  92.9 us
    dot_general x1, matrix products, body(): jnp.einsum('fzyx,xw->fzyw', fields, kernel_table, precision=highest)  59.5 us
    dot_general x1, matrix products, body(): jnp.einsum('fpyx,pi->fiyx', padded_z, band_table(z_local), precision=high...  58.4 us
    add x1, other arithmetic, body(): return level_set + dt_step * (nu_diff * laplace + dirac_weight * forcing)  38.8 us
    ppermute x4, waiting for transfers between devices, extended(): after = lax.ppermute(first, axis, down)  37.4 us
    dot_general x1, matrix products, body(): jnp.einsum('fzpx,pi->fzix', padded_y, band_table(y_local), precision=high...  35.3 us
    concatenate x1, other arithmetic, extended(): value = jnp.concatenate([before, value, after], axis=dim)  24.2 us
    dot_general x1, local copies, waits for them, and re-layouts, body(): jnp.einsum('fpyx,pi->fiyx', padded_z, band_table(z_local), precision=high...  16.7 us
  transfers between devices with their start and end apart: 8, of which 4 were waited for; matrix products, arithmetic and copies ran while one was open for 28% of the time, Pallas kernels for 0%

commit v1 on v0

v1 whole, which is shorter than its diff:
```python
import functools
import math

import jax
import jax.numpy as jnp
import numpy as np
from jax import lax
from jax.experimental import pallas as pl
from jax.experimental.pallas import tpu as pltpu
from jax.sharding import PartitionSpec as P

RADIUS = 6
SLAB = 8
EDGE = 8
TILE = 16
LANES = 128

sigma_cells = 8.0
dt_step = 0.5
nu_diff = 0.1
eps_fit = 0.05

ATAN_COEFS = (
    0.318309854, -0.106098923, 0.0635640505, -0.0446161759,
    0.0315320858, -0.0188971351, 0.00769233704, -0.0014861167,
)
TAP_SCALE = 0.519


def taps():
    d = np.arange(RADIUS + 1, dtype=np.float64)
    exact = np.exp(-d * d / (2.0 * sigma_cells * sigma_cells))
    short = np.asarray((TAP_SCALE * exact).astype(np.float32).astype(jnp.bfloat16))
    short64 = short.astype(np.float64)
    short_sum = short64[0] + 2.0 * short64[1:].sum()
    z_taps = exact / (exact[0] + 2.0 * exact[1:].sum()) / (short_sum * short_sum)
    return [float(v) for v in z_taps], short


def band(out_pos, in_pos, period=None):
    _, short = taps()
    dist = np.abs(out_pos[:, None] - in_pos[None, :])
    if period is not None:
        dist = np.minimum(dist, period - dist)
    table = np.where(dist <= RADIUS, short.astype(np.float32)[np.minimum(dist, RADIUS)], 0.0)
    return jnp.asarray(table.astype(np.float32), jnp.bfloat16)


def heaviside(x):
    far = jnp.abs(x) > 1.0
    t = jnp.where(far, 1.0 / x, x)
    z = t * t
    p = ATAN_COEFS[-1]
    for c in ATAN_COEFS[-2::-1]:
        p = p * z + c
    p = p * t
    base = jnp.where(far, jnp.where(x > 0.0, 1.0, 0.0), 0.5)
    return base + jnp.where(far, -p, p)


def part_kernel(plan, *refs):
    n_in = len(plan["inputs"])
    srcs = refs[:n_in]
    wy_ref, wx_ref = refs[n_in], refs[n_in + 1]
    pos = n_in + 2 + (1 if plan["aliased"] else 0)
    out_ref = refs[pos]
    lev, img, hea, zb, xb, xr, ob, in_sem, out_sem = refs[pos + 1 :]
    rows, rows_out, length = plan["rows"], plan["rows_out"], plan["length"]
    groups, slabs = plan["groups"], plan["slabs"]
    z_taps, _ = taps()

    copies = []
    for k, (which, src_index, dst_index) in enumerate(plan["copies"]):
        for f, dst in enumerate((lev, img)):
            src = srcs[which[f]]
            for axis_lead in src_index[f][0]:
                src = src.at[axis_lead]
            src = src.at[tuple(pl.ds(a, n) for a, n in src_index[f][1])]
            copy = pltpu.make_async_copy(
                src, dst.at[tuple(pl.ds(a, n) for a, n in dst_index)], in_sem.at[2 * k + f]
            )
            copy.start()
            copies.append(copy)
    for copy in copies:
        copy.wait()

    def fill(z, carry):
        hea[z] = heaviside(lev[z])
        return carry

    lax.fori_loop(plan["z_used"][0], plan["z_used"][1], fill, 0)

    def slab(s, carry):
        first = plan["slab_start"](s)

        def along_z(r, c):
            at = pl.multiple_of(r * TILE, TILE)
            for lane in range(0, length, LANES):
                for f in range(4):
                    vals = []
                    for z in range(SLAB + 2 * RADIUS):
                        where = (first + z, pl.ds(at, TILE), pl.ds(lane, LANES))
                        if f == 0:
                            v = hea[where] * img[where]
                        elif f == 1:
                            v = hea[where]
                        elif f == 2:
                            v = img[where]
                        else:
                            v = img[where]
                            v = v * v
                        vals.append(v)
                    for z in range(SLAB):
                        acc = vals[z + RADIUS] * z_taps[0]
                        for d in range(1, RADIUS + 1):
                            acc = acc + (vals[z + RADIUS - d] + vals[z + RADIUS + d]) * z_taps[d]
                        hi = acc.astype(jnp.bfloat16)
                        lo = (acc - hi.astype(jnp.float32)).astype(jnp.bfloat16)
                        cols = pl.ds(f * length + lane, LANES)
                        zb[z, pl.ds(at, TILE), cols] = hi
                        zb[z, pl.ds(at + rows, TILE), cols] = lo
            return c

        lax.fori_loop(0, rows // TILE, along_z, 0)

        def along_yx(z, c):
            for f in range(4):
                acc = jnp.dot(
                    wy_ref[...], zb[z, :, f * length : (f + 1) * length],
                    preferred_element_type=jnp.float32,
                )
                hi = acc.astype(jnp.bfloat16)
                lo = (acc - hi.astype(jnp.float32)).astype(jnp.bfloat16)
                xb[f * rows_out : (f + 1) * rows_out, :length] = hi
                xb[f * rows_out : (f + 1) * rows_out, length:] = lo
            xr[...] = jnp.dot(xb[...], wx_ref[...], preferred_element_type=jnp.float32)
            zi = first + RADIUS + z
            row = 0
            for start, count, _ in groups:
                for i in range(0, count, 8):
                    s1, s2, s3, s4 = (
                        xr[f * rows_out + row + i : f * rows_out + row + i + 8, :] for f in range(4)
                    )
                    at = start + i
                    lv = lev[zi, at : at + 8, :]
                    im = img[zi, at : at + 8, :]
                    inner = s2 + eps_fit
                    outer = (1.0 + eps_fit) - s2
                    spread = s4 - s3 * s3 + eps_fit
                    left = s1 * outer
                    right = (s3 - s1) * inner
                    prod = inner * outer
                    denom = (prod * prod) * (spread * (math.pi * (1.0 + lv * lv)))
                    numer = (left - right) * (2.0 * im * prod - (left + right))
                    laplace = (
                        (lev[zi - 1, at : at + 8, :] + lev[zi + 1, at : at + 8, :])
                        + (lev[zi, at - 1 : at + 7, :] + lev[zi, at + 1 : at + 9, :])
                        + (pltpu.roll(lv, 1, 1) + pltpu.roll(lv, length - 1, 1))
                        - 6.0 * lv
                    )
                    ob[s, z, row + i : row + i + 8, :] = lv + dt_step * (
                        nu_diff * laplace + numer / denom
                    )
                row += count
            return c

        lax.fori_loop(0, SLAB, along_yx, 0)
        row = 0
        for g, (_, count, y0) in enumerate(groups):
            pltpu.make_async_copy(
                ob.at[s, :, pl.ds(row, count), :],
                out_ref.at[pl.ds(plan["slab_out"](s), SLAB), pl.ds(y0, count), :],
                out_sem.at[s, g],
            ).start()
            row += count
        return carry

    lax.fori_loop(0, slabs, slab, 0)
    for s in range(slabs):
        row = 0
        for g, (_, count, y0) in enumerate(groups):
            pltpu.make_async_copy(
                ob.at[s, :, pl.ds(row, count), :],
                out_ref.at[pl.ds(plan["slab_out"](s), SLAB), pl.ds(y0, count), :],
                out_sem.at[s, g],
            ).wait()
            row += count


def run_part(plan, shape, srcs, wy, wx, prev):
    rows, rows_out, length, planes = plan["rows"], plan["rows_out"], plan["length"], plan["planes"]
    slabs = plan["slabs"]
    plan = dict(plan, inputs=srcs, aliased=prev is not None)
    any_spec = pl.BlockSpec(memory_space=pl.ANY)
    vmem = pl.BlockSpec(memory_space=pltpu.VMEM)
    args = list(srcs) + [wy, wx] + ([] if prev is None else [prev])
    specs = [any_spec] * len(srcs) + [vmem, vmem] + ([] if prev is None else [any_spec])
    n_out = slabs * SLAB * rows_out * length
    return pl.pallas_call(
        functools.partial(part_kernel, plan),
        out_shape=jax.ShapeDtypeStruct(shape, jnp.float32),
        in_specs=specs,
        out_specs=any_spec,
        scratch_shapes=[
            pltpu.VMEM((planes, rows, length), jnp.float32),
            pltpu.VMEM((planes, rows, length), jnp.float32),
            pltpu.VMEM((planes, rows, length), jnp.float32),
            pltpu.VMEM((SLAB, 2 * rows, 4 * length), jnp.bfloat16),
            pltpu.VMEM((4 * rows_out, 2 * length), jnp.bfloat16),
            pltpu.VMEM((4 * rows_out, length), jnp.float32),
            pltpu.VMEM((slabs, SLAB, rows_out, length), jnp.float32),
            pltpu.SemaphoreType.DMA((2 * len(plan["copies"]),)),
            pltpu.SemaphoreType.DMA((slabs, len(plan["groups"]))),
        ],
        input_output_aliases={} if prev is None else {len(args) - 1: 0},
        compiler_params=pltpu.CompilerParams(vmem_limit_bytes=60 * 1024 * 1024),
        cost_estimate=pl.CostEstimate(
            flops=n_out * 12000, bytes_accessed=n_out * 12, transcendentals=0
        ),
        name=plan["name"],
    )(*args)


def neighbours(axis):
    n = lax.axis_size(axis)
    up = [(i, (i + 1) % n) for i in range(n)]
    return up, [(j, i) for i, j in up]


def body(level_set, image):
    zl, yl, length = level_set.shape
    shape = level_set.shape
    r = RADIUS
    both = jnp.stack([level_set, image])
    y_up, y_down = neighbours("row")
    z_up, z_down = neighbours("col")

    y_before = lax.ppermute(both[:, :, yl - r :, :].transpose(0, 2, 1, 3), "row", y_up)
    y_after = lax.ppermute(both[:, :, :r, :].transpose(0, 2, 1, 3), "row", y_down)
    z_before = lax.ppermute(both[:, zl - r :], "col", z_up)
    z_after = lax.ppermute(both[:, :r], "col", z_down)

    y_rows = np.arange(yl)
    wx1 = band(np.arange(length), np.arange(length), length)
    wx = jnp.concatenate([wx1, wx1], axis=0)

    def doubled(out_pos, in_pos):
        w = band(out_pos, in_pos)
        return jnp.concatenate([w, w], axis=1)

    def block(lead, *ranges):
        return (lead, ranges)

    full = block((), (0, zl), (0, yl), (0, length))
    inner_slabs = (zl - 2 * EDGE) // SLAB
    interior = dict(
        name="interior", rows=yl, rows_out=yl - 2 * EDGE, length=length, planes=zl,
        slabs=inner_slabs, z_used=(EDGE - r, zl - EDGE + r),
        slab_start=lambda s: EDGE - r + SLAB * s, slab_out=lambda s: EDGE + SLAB * s,
        groups=((EDGE, yl - 2 * EDGE, EDGE),),
        copies=[((0, 1), (full, full), full[1])],
    )
    out = run_part(
        interior, shape, [level_set, image],
        doubled(y_rows[EDGE : yl - EDGE], y_rows), wx, None,
    )

    edge_last = jnp.stack([y_before[:, :, zl - r :], y_after[:, :, zl - r :]])
    edge_first = jnp.stack([y_before[:, :, :r], y_after[:, :, :r]])
    corner_before = lax.ppermute(edge_last, "col", z_up)
    corner_after = lax.ppermute(edge_first, "col", z_down)

    def strips(before, after):
        top = jnp.pad(before.transpose(0, 2, 1, 3), ((0, 0), (0, 0), (EDGE - r, 0), (0, 0)))
        low = jnp.pad(after.transpose(0, 2, 1, 3), ((0, 0), (0, 0), (0, EDGE - r), (0, 0)))
        return jnp.stack([top, low])

    y_strips = strips(y_before, y_after)
    inner = 2 * EDGE
    half = EDGE + inner

    def pair(lead_of, ranges):
        return tuple((lead_of(f), ranges) for f in range(2))

    y_edges = dict(
        name="y_edges", rows=2 * half, rows_out=2 * EDGE, length=length, planes=zl,
        slabs=inner_slabs, z_used=(EDGE - r, zl - EDGE + r),
        slab_start=lambda s: EDGE - r + SLAB * s, slab_out=lambda s: EDGE + SLAB * s,
        groups=((EDGE, EDGE, 0), (half + EDGE, EDGE, yl - EDGE)),
        copies=[
            ((2, 2), pair(lambda f: (0, f), ((0, zl), (0, EDGE), (0, length))),
             ((0, zl), (0, EDGE), (0, length))),
            ((0, 1), pair(lambda f: (), ((0, zl), (0, inner), (0, length))),
             ((0, zl), (EDGE, inner), (0, length))),
            ((0, 1), pair(lambda f: (), ((0, zl), (yl - inner, inner), (0, length))),
             ((0, zl), (half, inner), (0, length))),
            ((2, 2), pair(lambda f: (1, f), ((0, zl), (0, EDGE), (0, length))),
             ((0, zl), (half + inner, EDGE), (0, length))),
        ],
    )
    out_pos = np.concatenate([y_rows[:EDGE], y_rows[yl - EDGE :]])
    in_pos = np.concatenate([np.arange(-EDGE, inner), np.arange(yl - inner, yl + EDGE)])
    out = run_part(
        y_edges, shape, [level_set, image, y_strips], doubled(out_pos, in_pos), wx, out
    )

    corner_strips = jnp.stack(
        [strips(corner_before[0], corner_before[1]), strips(corner_after[0], corner_after[1])]
    )
    depth = SLAB + 2 * r
    near = depth - r
    copies = []
    for side, (z_halo, z_dst, local_src, local_dst) in enumerate(
        ((4, 0, 0, r), (5, depth + near, zl - near, depth))
    ):
        copies += [
            ((z_halo, z_halo), pair(lambda f: (f,), ((0, r), (0, yl), (0, length))),
             ((z_dst, r), (EDGE, yl), (0, length))),
            ((0, 1), pair(lambda f: (), ((local_src, near), (0, yl), (0, length))),
             ((local_dst, near), (EDGE, yl), (0, length))),
        ]
        for t, row in ((0, 0), (1, EDGE + yl)):
            copies += [
                ((2, 2), pair(lambda f, t=t: (t, f), ((local_src, near), (0, EDGE), (0, length))),
                 ((local_dst, near), (row, EDGE), (0, length))),
                ((3, 3),
                 pair(lambda f, t=t, side=side: (side, t, f), ((0, r), (0, EDGE), (0, length))),
                 ((z_dst, r), (row, EDGE), (0, length))),
            ]
    z_edges = dict(
        name="z_edges", rows=yl + 2 * EDGE, rows_out=yl, length=length, planes=2 * depth,
        slabs=2, z_used=(0, 2 * depth),
        slab_start=lambda s: depth * s, slab_out=lambda s: (zl - EDGE) * s,
        groups=((EDGE, yl, 0),),
        copies=copies,
    )
    return run_part(
        z_edges, shape,
        [level_set, image, y_strips, corner_strips, z_before, z_after],
        doubled(y_rows, np.arange(-EDGE, yl + EDGE)), wx, out,
    )


def solution(mesh):
    return jax.shard_map(
        body,
        mesh=mesh,
        in_specs=(P("col", "row", None), P("col", "row", None)),
        out_specs=P("col", "row", None),
        check_vma=False,
    )
```

time: 424 us -> 133 us (0.31); the launches traced: 419 us -> 133 us
  matrix products: 153 us -> 0 us
  waiting for transfers between devices: 130 us -> 0.02 us
  Pallas kernels: 0 us -> 111 us
  other arithmetic: 82.7 us -> 5.42 us
  local copies, waits for them, and re-layouts: 40.2 us -> 6.48 us
    dot_general x3 -> x0, matrix products: 153 us -> none  [the longest x1 59.5 us: body(): jnp.einsum('fzyx,xw->fzyw', fields, kernel_table, precision=highest)]
    ppermute x8 -> x6, waiting for transfers between devices: 130 us -> 0.02 us  [the longest x1 0.01 us: body(): lax.ppermute(both[:, :, :r, :].transpose(0, 2, 1, 3), 'row', y_down)]
    pallas_call x0 -> x3, Pallas kernels: none -> 111 us  [run_part(): pl.pallas_call(functools.partial(part_kernel, plan), out_shape=jax.ShapeD...]
    add x1 -> x0, other arithmetic: 38.8 us -> none  [body(): return level_set + dt_step * (nu_diff * laplace + dirac_weight * forcing)]
    concatenate x1 -> x0, other arithmetic: 24.2 us -> none  [extended(): value = jnp.concatenate([before, value, after], axis=dim)]
    slice x7 -> x0, local copies, waits for them, and re-layouts: 22.3 us -> none  [the longest x2 15.1 us: body(): jnp.roll(level_set, -1, 2)]
    dot_general x1 -> x0, local copies, waits for them, and re-layouts: 16.7 us -> none  [body(): jnp.einsum('fpyx,pi->fiyx', padded_z, band_table(z_local), precision=high...]
    another operation x1 -> x7, other arithmetic: 16.4 us -> 3.51 us  [the longest x1 1.57 us: strips(): return jnp.stack([top, low])]
  transfers between devices with their start and end apart: 8 -> 6, of which waited for: 4 -> 0; matrix products, arithmetic and copies ran while one was open for 28% -> 7% of each run, Pallas kernels for 0% -> 58%
where the time goes in v1:
time: 133 us
  Pallas kernels  111 us (83%)
  starting transfers between devices  9.44 us (7%)
  local copies, waits for them, and re-layouts  6.48 us (5%)
  other arithmetic  5.42 us (4%)
    pallas_call x3, Pallas kernels, run_part(): pl.pallas_call(functools.partial(part_kernel, plan), out_shape=jax.ShapeD...  111 us
    ppermute x1, starting transfers between devices, body(): lax.ppermute(both[:, :, :r, :].transpose(0, 2, 1, 3), 'row', y_down)  5.09 us
  transfers between devices with their start and end apart: 6, of which 0 were waited for; matrix products, arithmetic and copies ran while one was open for 7% of the time, Pallas kernels for 58%

profile of v1, /device:TPU:0, one launch (start us, length us, event | category | flops | bytes accessed | tf_op | source)
XLA Modules:
  0.0 132.6 jit_solution(6124273557798790389)
XLA Ops:
  0.0 0.0 slice-start
  0.0 0.0 slice-start.2
  0.0 1.9 %maximum_bitcast_fusion.1 = (f32[2,6,48,384]{3,1,2,0:T(8,128)S(1)}, f32[2,6,48,384]{3,1,2,0:T(8,128)S(1)}) fusion(f32[1,48,96,384]{3,2,1,0:T(8,128)} %bitcast.54, f32[1,48,96,384]{3,2,1,0:T(8,128)} %bitcast.50), kind=kLoop, calls=%fused_computation.4 | loop fusion | flops 442368 | bytes 15925248 | tf_op jit(solution)/shard_map/transpose | solution.py:238
  1.9 1.1 copy.11
  3.0 5.1 %collective-permute-start.1 = (f32[2,6,48,384]{3,2,1,0:T(8,128)}, f32[2,6,48,384]{3,2,1,0:T(8,128)}, u32[]{:S(2)}, u32[]{:S(2)}) collective-permute-start(f32[2,6,48,384]{3,2,1,0:T(8,128)} %copy.11), channel_id=1, source_target_pairs={{8,0},{16,8},{24,16},{0,24},{9,1},{17,9},{25,17},{1,25},{10,2},{18... | collective-permute-start | bytes 2654216 | tf_op jit(solution)/shard_map/ppermute | solution.py:239
  8.1 1.1 copy.9
  9.2 0.0 collective-permute-start
  9.2 0.0 slice-done
  9.2 0.0 slice-done.2
  9.2 0.0 slice-done.1
  9.2 0.0 slice-done.3
  9.3 0.2 pad_maximum_fusion.1
  9.5 1.7 %collective-permute-start.5 = (f32[2,6,96,384]{3,2,1,0:T(8,128)S(1)}, f32[2,6,96,384]{3,2,1,0:T(8,128)}, u32[]{:S(2)}, u32[]{:S(2)}) collective-permute-start(f32[2,6,96,384]{3,2,1,0:T(8,128)S(1)} %get-tuple-element.5), channel_id=1, source_target_pairs={{1,0},{2,1},{3,2},{4,3},{5,4},{6,5},{7,6},{0,7},{9,8},{10,9},{11,1... | collective-permute-start | bytes 5308424 | tf_op jit(solution)/shard_map/ppermute | solution.py:241
  11.2 0.0 collective-permute-start.4
  11.2 49.8 %interior.1.refs_5_ = f32[48,96,384]{2,1,0:T(8,128)} custom-call(f32[48,96,384]{2,1,0:T(8,128)} %refs_0_.5, f32[48,96,384]{2,1,0:T(8,128)} %refs_1_.5, bf16[80,192]{1,0:T(8,128)(2,1)} %constant.30.refs_2_, bf16[768,384]{1,0:T(8,128)(2,1)} %constant.28.refs_3_.refs_4_.refs_7_), custom_call_target="tpu_custom_call" | custom-call | flops 11796480000 | bytes 11796480 | tf_op jit(solution)/shard_map/interior/pallas_call | solution.py:199
  60.9 0.0 collective-permute-done.1
  60.9 1.4 %copy.22 = f32[2,6,48,384]{3,1,2,0:T(8,128)S(1)} copy(f32[2,6,48,384]{3,2,1,0:T(8,128)} %collective-permute-done.1) | data formatting | bytes 1769472 | tf_op jit(solution)/shard_map/ppermute | solution.py:239
  62.4 0.0 collective-permute-done
  62.4 1.4 %copy.21 = f32[2,6,48,384]{3,1,2,0:T(8,128)S(1)} copy(f32[2,6,48,384]{3,2,1,0:T(8,128)} %collective-permute-done) | data formatting | bytes 1769472 | tf_op jit(solution)/shard_map/ppermute | solution.py:238
  63.9 0.7 pad_maximum_fusion.5
  64.6 2.6 %collective-permute-start.3 = (f32[2,2,6,6,384]{4,2,3,1,0:T(8,128)}, f32[2,2,6,6,384]{4,2,3,1,0:T(8,128)}, u32[]{:S(2)}, u32[]{:S(2)}) collective-permute-start(f32[2,2,6,6,384]{4,2,3,1,0:T(8,128)} %pad_maximum_fusion.5), channel_id=1, source_target_pairs={{1,0},{2,1},{3,2},{4,3},{5,4},{6,5},{7,6},{0,7},{9,8},{10,9},{11,1... | collective-permute-start | bytes 663560 | tf_op jit(solution)/shard_map/ppermute | solution.py:271
  67.3 0.1 collective-permute-start.2
  67.4 0.2 pad_bitcast_fusion
  67.6 1.6 %pad_maximum_fusion.refs_2_ = f32[2,2,48,8,384]{4,3,2,1,0:T(8,128)} fusion(f32[1,2,48,8,384]{4,3,2,1,0:T(8,128)S(1)} %get-tuple-element.21, f32[1,2,48,8,384]{4,3,2,1,0:T(8,128)S(1)} %get-tuple-element.22), kind=kLoop, calls=%fused_computation | loop fusion | flops 589824 | bytes 4718592 | tf_op jit(solution)/shard_map/stack | solution.py:276
  69.2 27.5 %y_edges.1.refs_8_ = f32[48,96,384]{2,1,0:T(8,128)} custom-call(f32[48,96,384]{2,1,0:T(8,128)} %refs_0_.5, f32[48,96,384]{2,1,0:T(8,128)} %refs_1_.5, f32[2,2,48,8,384]{4,3,2,1,0:T(8,128)} %pad_maximum_fusion.refs_2_, bf16[16,96]{1,0:T(8,128)(2,1)} %constant.29.refs_3_, ...), custom_call_target="tpu_custom_call", output_to_operand_aliasing={{}: (5, {})} | custom-call | flops 2359296000 | bytes 2359296 | tf_op jit(solution)/shard_map/y_edges/pallas_call | solution.py:199
  96.7 0.0 collective-permute-done.3
  96.7 1.0 slice_bitcast_fusion.1
  97.8 0.0 collective-permute-done.2
  97.9 0.9 pad_maximum_fusion.3.refs_3_
  98.8 0.0 collective-permute-done.5.refs_5_
  98.8 0.0 collective-permute-done.4.refs_4_
  98.8 33.8 %z_edges.1 = f32[48,96,384]{2,1,0:T(8,128)} custom-call(f32[48,96,384]{2,1,0:T(8,128)} %refs_0_.5, f32[48,96,384]{2,1,0:T(8,128)} %refs_1_.5, f32[2,2,48,8,384]{4,3,2,1,0:T(8,128)} %pad_maximum_fusion.refs_2_, f32[2,2,2,6,8,384]{5,4,3,2,1,0:T(8,128)} %pad_maximum_fusion.3.refs_3_, ...), custom_call_target="tpu_custom_call", output_to_operand_aliasing={{}: (8, {})} | custom-call | flops 7077888000 | bytes 7077888 | tf_op jit(solution)/shard_map/z_edges/pallas_call | solution.py:199
  (13 shorter events, 0.2 us)
Async XLA Ops:
  0.0 9.2 %slice-start = ((s8[7077888]{0:T(1024)(128)(4,1)}), s8[4194304]{0:T(1024)(128)(4,1)S(1)}, s32[]{:S(2)}) async-start(s8[7077888]{0:T(1024)(128)(4,1)} %bitcast.51), calls=%async_computation | async-start | bytes 8388608
  0.0 9.2 %slice-start.2 = ((s8[7077888]{0:T(1024)(128)(4,1)}), s8[4194304]{0:T(1024)(128)(4,1)S(1)}, s32[]{:S(2)}) async-start(s8[7077888]{0:T(1024)(128)(4,1)} %bitcast.55), calls=%async_computation.2 | async-start | bytes 8388608
  0.0 9.2 %slice-start.1 = ((s8[7077888]{0:T(1024)(128)(4,1)}), s8[2883584]{0:T(1024)(128)(4,1)S(1)}, s32[]{:S(2)}) async-start(s8[7077888]{0:T(1024)(128)(4,1)} %bitcast.51), calls=%async_computation.1 | async-start | bytes 5767168
  0.0 9.2 %slice-start.3 = ((s8[7077888]{0:T(1024)(128)(4,1)}), s8[2883584]{0:T(1024)(128)(4,1)S(1)}, s32[]{:S(2)}) async-start(s8[7077888]{0:T(1024)(128)(4,1)} %bitcast.55), calls=%async_computation.3 | async-start | bytes 5767168
  3.0 57.9 %collective-permute-start.1 = (f32[2,6,48,384]{3,2,1,0:T(8,128)}, f32[2,6,48,384]{3,2,1,0:T(8,128)}, u32[]{:S(2)}, u32[]{:S(2)}) collective-permute-start(f32[2,6,48,384]{3,2,1,0:T(8,128)} %copy.11), channel_id=1, source_target_pairs={{8,0},{16,8},{24,16},{0,24},{9,1},{17,9},{25,17},{1,25},{10,2},{18... | collective-permute-start | bytes 2654216 | tf_op jit(solution)/shard_map/ppermute | solution.py:239
  9.2 53.2 %collective-permute-start = (f32[2,6,48,384]{3,2,1,0:T(8,128)}, f32[2,6,48,384]{3,2,1,0:T(8,128)}, u32[]{:S(2)}, u32[]{:S(2)}) collective-permute-start(f32[2,6,48,384]{3,2,1,0:T(8,128)} %copy.9), channel_id=1, source_target_pairs={{0,8},{8,16},{16,24},{24,0},{1,9},{9,17},{17,25},{25,1},{2,10},{10... | collective-permute-start | bytes 2654216 | tf_op jit(solution)/shard_map/ppermute | solution.py:238
  9.5 89.3 %collective-permute-start.5 = (f32[2,6,96,384]{3,2,1,0:T(8,128)S(1)}, f32[2,6,96,384]{3,2,1,0:T(8,128)}, u32[]{:S(2)}, u32[]{:S(2)}) collective-permute-start(f32[2,6,96,384]{3,2,1,0:T(8,128)S(1)} %get-tuple-element.5), channel_id=1, source_target_pairs={{1,0},{2,1},{3,2},{4,3},{5,4},{6,5},{7,6},{0,7},{9,8},{10,9},{11,1... | collective-permute-start | bytes 5308424 | tf_op jit(solution)/shard_map/ppermute | solution.py:241
  11.2 87.6 %collective-permute-start.4 = (f32[2,6,96,384]{3,2,1,0:T(8,128)S(1)}, f32[2,6,96,384]{3,2,1,0:T(8,128)}, u32[]{:S(2)}, u32[]{:S(2)}) collective-permute-start(f32[2,6,96,384]{3,2,1,0:T(8,128)S(1)} %get-tuple-element.6), channel_id=1, source_target_pairs={{0,1},{1,2},{2,3},{3,4},{4,5},{5,6},{6,7},{7,0},{8,9},{9,10},{10,1... | collective-permute-start | bytes 5308424 | tf_op jit(solution)/shard_map/ppermute | solution.py:240
  64.6 32.1 %collective-permute-start.3 = (f32[2,2,6,6,384]{4,2,3,1,0:T(8,128)}, f32[2,2,6,6,384]{4,2,3,1,0:T(8,128)}, u32[]{:S(2)}, u32[]{:S(2)}) collective-permute-start(f32[2,2,6,6,384]{4,2,3,1,0:T(8,128)} %pad_maximum_fusion.5), channel_id=1, source_target_pairs={{1,0},{2,1},{3,2},{4,3},{5,4},{6,5},{7,6},{0,7},{9,8},{10,9},{11,1... | collective-permute-start | bytes 663560 | tf_op jit(solution)/shard_map/ppermute | solution.py:271
  67.3 30.5 %collective-permute-start.2 = (f32[2,2,6,6,384]{4,2,3,1,0:T(8,128)S(1)}, f32[2,2,6,6,384]{4,2,3,1,0:T(8,128)S(1)}, u32[]{:S(2)}, u32[]{:S(2)}) collective-permute-start(f32[2,2,6,6,384]{4,2,3,1,0:T(8,128)S(1)} %pad_maximum_fusion.4), channel_id=1, source_target_pairs={{0,1},{1,2},{2,3},{3,4},{4,5},{5,6},{6,7},{7,0},{8,9},{9,10},{10,1... | collective-permute-start | bytes 663560 | tf_op jit(solution)/shard_map/ppermute | solution.py:270

commit v2 on v0

v2 whole, which is shorter than its diff:
```python
import functools
import math

import jax
import jax.numpy as jnp
import numpy as np
from jax import lax
from jax.experimental import pallas as pl
from jax.experimental.pallas import tpu as pltpu
from jax.sharding import PartitionSpec as P

RADIUS = 6
PAIR = 2
EDGE = 8
TILE = 16
LANES = 128

sigma_cells = 8.0
dt_step = 0.5
nu_diff = 0.1
eps_fit = 0.05

ATAN_COEFS = (
    0.318309854, -0.106098923, 0.0635640505, -0.0446161759,
    0.0315320858, -0.0188971351, 0.00769233704, -0.0014861167,
)
TAP_SCALE = 0.519


def taps():
    d = np.arange(RADIUS + 1, dtype=np.float64)
    exact = np.exp(-d * d / (2.0 * sigma_cells * sigma_cells))
    short = np.asarray((TAP_SCALE * exact).astype(np.float32).astype(jnp.bfloat16))
    short64 = short.astype(np.float64)
    short_sum = short64[0] + 2.0 * short64[1:].sum()
    z_taps = exact / (exact[0] + 2.0 * exact[1:].sum()) / (short_sum * short_sum)
    return [float(v) for v in z_taps], short


def band(out_pos, in_pos, period=None):
    _, short = taps()
    dist = np.abs(out_pos[:, None] - in_pos[None, :])
    if period is not None:
        dist = np.minimum(dist, period - dist)
    table = np.where(dist <= RADIUS, short.astype(np.float32)[np.minimum(dist, RADIUS)], 0.0)
    return jnp.asarray(table.astype(np.float32), jnp.bfloat16)


def heaviside(x):
    far = jnp.abs(x) > 1.0
    t = jnp.where(far, 1.0 / x, x)
    z = t * t
    p = ATAN_COEFS[-1]
    for c in ATAN_COEFS[-2::-1]:
        p = p * z + c
    p = p * t
    base = jnp.where(far, jnp.where(x > 0.0, 1.0, 0.0), 0.5)
    return base + jnp.where(far, -p, p)


def interleave(first, second):
    a, b = len(first), len(second)
    done = 0
    for i, piece in enumerate(first):
        piece()
        want = (i + 1) * b // a
        while done < want:
            second[done]()
            done += 1


def split_bf16(acc):
    hi = acc.astype(jnp.bfloat16)
    return hi, (acc - hi.astype(jnp.float32)).astype(jnp.bfloat16)


def part_kernel(plan, *refs):
    srcs, wys, wx_ref, _, outs, scratch = plan["unpack"](refs)
    out_ref = outs[0]
    lev, img, hea, him, sqr, zb0, zb1, xb, xr, ob, in_sem, out_sem, exp_sem = scratch[:13]
    rows, rows_out, length = plan["rows"], plan["rows_out"], plan["length"]
    groups, steps = plan["groups"], plan["steps"]
    z_taps, _ = taps()
    fields = (him, hea, img, sqr)

    def copy_in(k):
        src, lead, src_ranges, dst, dst_ranges = plan["copies"][k]
        src = srcs[src]
        for i in lead:
            src = src.at[i]
        return pltpu.make_async_copy(
            src.at[tuple(pl.ds(a, n) for a, n in src_ranges)],
            scratch[dst].at[tuple(pl.ds(a, n) for a, n in dst_ranges)],
            in_sem.at[k],
        )

    for k in range(len(plan["copies"])):
        copy_in(k).start()

    def fill(z, carry, spans):
        for a, n, compute in spans:
            if compute:
                hea[z, a : a + n, :] = heaviside(lev[z, a : a + n, :])
            im = img[z, a : a + n, :]
            him[z, a : a + n, :] = hea[z, a : a + n, :] * im
            sqr[z, a : a + n, :] = im * im
        return carry

    for waits, (z0, z1), spans in plan["fills"]:
        for k in waits:
            copy_in(k).wait()
        lax.fori_loop(z0, z1, functools.partial(fill, spans=spans), 0)

    exports = []
    for e, (a, n) in enumerate(plan["h_export"]):
        copy = pltpu.make_async_copy(
            hea.at[pl.ds(a, n)], outs[1].at[pl.ds(a, n)], exp_sem.at[e]
        )
        copy.start()
        exports.append(copy)

    def z_tile(first, zb, at, lane, f):
        def emit():
            vals = [
                fields[f][first + z, pl.ds(at, TILE), pl.ds(lane, LANES)]
                for z in range(PAIR + 2 * RADIUS)
            ]
            for z in range(PAIR):
                acc = vals[z + RADIUS] * z_taps[0]
                for d in range(1, RADIUS + 1):
                    acc = acc + (vals[z + RADIUS - d] + vals[z + RADIUS + d]) * z_taps[d]
                hi, lo = split_bf16(acc)
                cols = pl.ds(f * length + lane, LANES)
                zb[z, pl.ds(at, TILE), cols] = hi
                zb[z, pl.ds(at + rows, TILE), cols] = lo

        return emit

    def z_pieces(first, zb, row_starts):
        return [
            z_tile(first, zb, at, lane, f)
            for at in row_starts
            for lane in range(0, length, LANES)
            for f in range(4)
        ]

    wide = 2 * LANES

    def along_y(t, z, zb, col):
        def emit():
            acc = jnp.dot(
                wys[0][...], zb[z, :, col : col + wide], preferred_element_type=jnp.float32
            )
            if plan["ready"]:
                acc = acc + jnp.dot(
                    wys[1][...], scratch[13][PAIR * t + z, :, col : col + wide],
                    preferred_element_type=jnp.float32,
                )
            hi, lo = split_bf16(acc)
            for part in range(0, wide, LANES):
                f, x = divmod(col + part, length)
                at = (z * 4 + f) * rows_out
                xb[at : at + rows_out, x : x + LANES] = hi[:, part : part + LANES]
                xb[at : at + rows_out, length + x : length + x + LANES] = lo[:, part : part + LANES]

        return emit

    def along_x(z):
        def emit():
            at = z * 4 * rows_out
            xr[at : at + 4 * rows_out, :] = jnp.dot(
                xb[at : at + 4 * rows_out, :], wx_ref[...], preferred_element_type=jnp.float32
            )

        return emit

    def update(t, z, zi, row, at):
        def emit():
            s1, s2, s3, s4 = (
                xr[(z * 4 + f) * rows_out + row : (z * 4 + f) * rows_out + row + 8, :]
                for f in range(4)
            )
            lv, im, before, after, above, below = plan["local"](scratch, zi, at)
            inner = s2 + eps_fit
            outer = (1.0 + eps_fit) - s2
            spread = s4 - s3 * s3 + eps_fit
            left = s1 * outer
            right = (s3 - s1) * inner
            prod = inner * outer
            denom = (prod * prod) * (spread * (math.pi * (1.0 + lv * lv)))
            numer = (left - right) * (2.0 * im * prod - (left + right))
            laplace = (
                (before + after)
                + (above + below)
                + (pltpu.roll(lv, 1, 1) + pltpu.roll(lv, length - 1, 1))
                - 6.0 * lv
            )
            ob[PAIR * t + z, row : row + 8, :] = lv + dt_step * (
                nu_diff * laplace + numer / denom
            )

        return emit

    def yxf_pieces(t, zb):
        zi = plan["base"](t) + RADIUS
        pieces = [
            along_y(t, z, zb, col) for z in range(PAIR) for col in range(0, 4 * length, wide)
        ]
        pieces += [along_x(z) for z in range(PAIR)]
        for z in range(PAIR):
            row = 0
            for start, count, _ in groups:
                pieces += [update(t, z, zi + z, row + i, start + i) for i in range(0, count, 8)]
                row += count
        return pieces

    def out_copies(t):
        row, made = 0, []
        for g, (_, count, y0) in enumerate(groups):
            made.append(
                pltpu.make_async_copy(
                    ob.at[pl.ds(PAIR * t, PAIR), pl.ds(row, count), :],
                    out_ref.at[pl.ds(plan["out_z"](t), PAIR), pl.ds(y0, count), :],
                    out_sem.at[t, g],
                )
            )
            row += count
        return made

    n_h = len(plan["h_export"])

    def z_export(t, zb, slot):
        return [
            pltpu.make_async_copy(
                zb.at[:, pl.ds(src, TILE), :],
                outs[2].at[pl.ds(PAIR * t, PAIR), pl.ds(TILE * e, TILE), :],
                exp_sem.at[n_h + len(plan["z_export"]) * slot + e],
            )
            for e, src in enumerate(plan["z_export"])
        ]

    def prologue(r, carry):
        at = pl.multiple_of(r * TILE, TILE)
        for piece in z_pieces(plan["base"](0), zb0, [at]):
            piece()
        return carry

    lax.fori_loop(0, rows // TILE, prologue, 0)
    for copy in z_export(0, zb0, 0):
        copy.start()
    for k in plan["late_waits"]:
        copy_in(k).wait()
    tiles = list(range(0, rows, TILE))

    def two_steps(i, carry):
        for half, (now, nxt) in enumerate(((zb0, zb1), (zb1, zb0))):
            t = 2 * i + half
            after = jnp.minimum(t + 1, steps - 1)
            if not plan["z_export"]:
                pass
            elif half == 0:
                @pl.when(i > 0)
                def _():
                    for copy in z_export(t - 1, nxt, 1):
                        copy.wait()
            else:
                for copy in z_export(t - 1, nxt, 0):
                    copy.wait()
            interleave(yxf_pieces(t, now), z_pieces(plan["base"](after), nxt, tiles))
            for copy in out_copies(t):
                copy.start()
            if not plan["z_export"]:
                pass
            elif half == 0:
                for copy in z_export(t + 1, nxt, 1):
                    copy.start()
            else:
                @pl.when(i + 1 < steps // 2)
                def _():
                    for copy in z_export(t + 1, nxt, 0):
                        copy.start()
        return carry

    lax.fori_loop(0, steps // 2, two_steps, 0)
    for copy in z_export(steps - 1, zb1, 1):
        copy.wait()
    for copy in exports:
        copy.wait()

    def finish(t, carry):
        for copy in out_copies(t):
            copy.wait()
        return carry

    lax.fori_loop(0, steps, finish, 0)


def run_part(plan, shape, srcs, wys, wx, prev):
    rows, rows_out, length, planes = plan["rows"], plan["rows_out"], plan["length"], plan["planes"]
    steps, n_ready = plan["steps"], plan.get("ready", 0)
    n_src, n_wy, n_out = len(srcs), len(wys), 1 + len(plan["extra_out"])
    n_prev = 0 if prev is None else 1

    def unpack(refs):
        cuts = np.cumsum([n_src, n_wy, 1, n_prev, n_out])
        a, b, c, d, e = (int(v) for v in cuts)
        return refs[:a], refs[a:b], refs[b], refs[c:d], refs[d:e], refs[e:]

    plan = dict(plan, unpack=unpack, ready=n_ready)
    any_spec = pl.BlockSpec(memory_space=pl.ANY)
    vmem = pl.BlockSpec(memory_space=pltpu.VMEM)
    args = list(srcs) + list(wys) + [wx] + ([] if prev is None else [prev])
    specs = [any_spec] * n_src + [vmem] * (n_wy + 1) + [any_spec] * n_prev
    n_elem = PAIR * steps * rows_out * length
    field = pltpu.VMEM((planes, rows, length), jnp.float32)
    taps_buffer = pltpu.VMEM((PAIR, 2 * rows, 4 * length), jnp.bfloat16)
    scratch = [field] * 5 + [
        taps_buffer,
        taps_buffer,
        pltpu.VMEM((PAIR * 4 * rows_out, 2 * length), jnp.bfloat16),
        pltpu.VMEM((PAIR * 4 * rows_out, length), jnp.float32),
        pltpu.VMEM((PAIR * steps, rows_out, length), jnp.float32),
        pltpu.SemaphoreType.DMA((len(plan["copies"]),)),
        pltpu.SemaphoreType.DMA((steps, len(plan["groups"]))),
        pltpu.SemaphoreType.DMA((max(1, len(plan["h_export"]) + 2 * len(plan["z_export"])),)),
    ]
    if n_ready:
        scratch += [
            pltpu.VMEM((PAIR * steps, n_ready, 4 * length), jnp.bfloat16),
            pltpu.VMEM((planes, 2 * (EDGE + TILE), length), jnp.float32),
            pltpu.VMEM((planes, 2 * (EDGE + TILE), length), jnp.float32),
        ]
    out = pl.pallas_call(
        functools.partial(part_kernel, plan),
        out_shape=[jax.ShapeDtypeStruct(shape, jnp.float32)] + plan["extra_out"],
        in_specs=specs,
        out_specs=[any_spec] * n_out,
        scratch_shapes=scratch,
        input_output_aliases={} if prev is None else {len(args) - 1: 0},
        compiler_params=pltpu.CompilerParams(vmem_limit_bytes=60 * 1024 * 1024),
        cost_estimate=pl.CostEstimate(
            flops=n_elem * 12000, bytes_accessed=n_elem * 12, transcendentals=0
        ),
        name=plan["name"],
    )(*args)
    return out


def neighbours(axis):
    n = lax.axis_size(axis)
    up = [(i, (i + 1) % n) for i in range(n)]
    return up, [(j, i) for i, j in up]


def local_of(lev_at, img_at):
    def local(scratch, zi, at):
        lev, img = scratch[lev_at], scratch[img_at]
        return (
            lev[zi, at : at + 8, :],
            img[zi, at : at + 8, :],
            lev[zi - 1, at : at + 8, :],
            lev[zi + 1, at : at + 8, :],
            lev[zi, at - 1 : at + 7, :],
            lev[zi, at + 1 : at + 9, :],
        )

    return local


LEV, IMG, HEA, READY, NEAR_LEV, NEAR_IMG = 0, 1, 2, 13, 14, 15


def body(level_set, image):
    zl, yl, length = level_set.shape
    shape = level_set.shape
    r = RADIUS
    both = jnp.stack([level_set, image])
    y_up, y_down = neighbours("row")
    z_up, z_down = neighbours("col")

    y_before = lax.ppermute(both[:, :, yl - r :, :].transpose(0, 2, 1, 3), "row", y_up)
    y_after = lax.ppermute(both[:, :, :r, :].transpose(0, 2, 1, 3), "row", y_down)
    z_before = lax.ppermute(both[:, zl - r :], "col", z_up)
    z_after = lax.ppermute(both[:, :r], "col", z_down)

    y_rows = np.arange(yl)
    wx1 = band(np.arange(length), np.arange(length), length)
    wx = jnp.concatenate([wx1, wx1], axis=0)

    def doubled(out_pos, in_pos):
        w = band(out_pos, in_pos)
        return jnp.concatenate([w, w], axis=1)

    def full(z0, zn, y0, yn):
        return ((z0, zn), (y0, yn), (0, length))

    depth = PAIR * 4 + 2 * r
    near = depth - r
    inner_steps = (zl - 2 * EDGE) // PAIR
    chunk = zl // 3
    interior = dict(
        name="interior", rows=yl, rows_out=yl - 2 * EDGE, length=length, planes=zl,
        steps=inner_steps,
        base=lambda t: EDGE - r + PAIR * t, out_z=lambda t: EDGE + PAIR * t,
        groups=((EDGE, yl - 2 * EDGE, EDGE),), local=local_of(LEV, IMG),
        copies=[
            (f, (), full(z, chunk, 0, yl), f, full(z, chunk, 0, yl))
            for z in range(0, zl, chunk) for f in (LEV, IMG)
        ],
        fills=[
            ((2 * c, 2 * c + 1), (c * chunk, (c + 1) * chunk), ((0, yl, True),)) for c in range(3)
        ],
        h_export=((0, near), (zl - near, near)),
        z_export=(0, yl - TILE, yl, 2 * yl - TILE),
        late_waits=(),
        extra_out=[
            jax.ShapeDtypeStruct(shape, jnp.float32),
            jax.ShapeDtypeStruct((PAIR * inner_steps, 4 * TILE, 4 * length), jnp.bfloat16),
        ],
    )
    out, hea, near_rows = run_part(
        interior, shape, [level_set, image],
        [doubled(y_rows[EDGE : yl - EDGE], y_rows)], wx, None,
    )

    edge_last = jnp.stack([y_before[:, :, zl - r :], y_after[:, :, zl - r :]])
    edge_first = jnp.stack([y_before[:, :, :r], y_after[:, :, :r]])
    corner_before = lax.ppermute(edge_last, "col", z_up)
    corner_after = lax.ppermute(edge_first, "col", z_down)

    def strips(before, after):
        top = jnp.pad(before.transpose(0, 2, 1, 3), ((0, 0), (0, 0), (EDGE - r, 0), (0, 0)))
        low = jnp.pad(after.transpose(0, 2, 1, 3), ((0, 0), (0, 0), (0, EDGE - r), (0, 0)))
        return jnp.stack([top, low])

    y_strips = strips(y_before, y_after)
    half = EDGE + TILE
    z_lo, z_n = EDGE - r, zl - 2 * (EDGE - r)
    copies = [
        (2, (side, f), full(z_lo, z_n, 0, EDGE), f, full(z_lo, z_n, side * EDGE, EDGE))
        for side in range(2) for f in (LEV, IMG)
    ]
    n_first = len(copies)
    for f, dst in ((0, NEAR_LEV), (1, NEAR_IMG)):
        copies += [
            (2, (0, f), full(z_lo, z_n, 0, EDGE), dst, full(z_lo, z_n, 0, EDGE)),
            (f, (), full(z_lo, z_n, 0, TILE), dst, full(z_lo, z_n, EDGE, TILE)),
            (f, (), full(z_lo, z_n, yl - TILE, TILE), dst, full(z_lo, z_n, half, TILE)),
            (2, (1, f), full(z_lo, z_n, 0, EDGE), dst, full(z_lo, z_n, half + TILE, EDGE)),
        ]
    ready_all = ((0, PAIR * inner_steps), (0, 4 * TILE), (0, 4 * length))
    copies.append((3, (), ready_all, READY, ready_all))
    y_edges = dict(
        name="y_edges", rows=2 * EDGE, rows_out=2 * EDGE, length=length, planes=zl,
        steps=inner_steps,
        base=lambda t: EDGE - r + PAIR * t, out_z=lambda t: EDGE + PAIR * t,
        groups=((EDGE, EDGE, 0), (half + EDGE, EDGE, yl - EDGE)),
        local=local_of(NEAR_LEV, NEAR_IMG),
        copies=copies,
        fills=[(tuple(range(n_first)), (z_lo, z_lo + z_n), ((0, 2 * EDGE, True),))],
        h_export=(), z_export=(), late_waits=tuple(range(n_first, len(copies))),
        extra_out=[], ready=4 * TILE,
    )
    out_pos = np.concatenate([y_rows[:EDGE], y_rows[yl - EDGE :]])
    halo_pos = np.concatenate([np.arange(-EDGE, 0), np.arange(yl, yl + EDGE)])
    near_pos = np.concatenate([np.arange(TILE), np.arange(yl - TILE, yl)])
    (out,) = run_part(
        y_edges, shape, [level_set, image, y_strips, near_rows],
        [doubled(out_pos, halo_pos), doubled(out_pos, near_pos)], wx, out,
    )

    corner_strips = jnp.stack(
        [strips(corner_before[0], corner_before[1]), strips(corner_after[0], corner_after[1])]
    )
    rows = yl + 2 * EDGE
    halo_copies, near_copies = [], []
    for side, (z_dst, src, dst) in enumerate(
        ((0, 0, r), (depth + near, zl - near, depth))
    ):
        near_copies.append((6, (), full(src, near, 0, yl), HEA, full(dst, near, EDGE, yl)))
        for f in (LEV, IMG):
            halo_copies.append(
                (4 + side, (f,), full(0, r, 0, yl), f, full(z_dst, r, EDGE, yl))
            )
            near_copies.append((f, (), full(src, near, 0, yl), f, full(dst, near, EDGE, yl)))
            for t, row in ((0, 0), (1, EDGE + yl)):
                halo_copies.append(
                    (3, (side, t, f), full(0, r, 0, EDGE), f, full(z_dst, r, row, EDGE))
                )
                near_copies.append(
                    (2, (t, f), full(src, near, 0, EDGE), f, full(dst, near, row, EDGE))
                )
    copies = halo_copies + near_copies
    whole = ((0, rows, True),)
    z_edges = dict(
        name="z_edges", rows=rows, rows_out=yl, length=length, planes=2 * depth, steps=8,
        base=lambda t: depth * (t // 4) + PAIR * (t % 4),
        out_z=lambda t: (zl - EDGE) * (t // 4) + PAIR * (t % 4),
        groups=((EDGE, yl, 0),), local=local_of(LEV, IMG),
        copies=copies,
        fills=[
            (tuple(range(len(halo_copies))), (0, r), whole),
            ((), (depth + near, 2 * depth), whole),
            (
                tuple(range(len(halo_copies), len(copies))), (r, depth + near),
                ((0, EDGE, True), (EDGE, yl, False), (EDGE + yl, EDGE, True)),
            ),
        ],
        h_export=(), z_export=(), late_waits=(), extra_out=[],
    )
    (out,) = run_part(
        z_edges, shape,
        [level_set, image, y_strips, corner_strips, z_before, z_after, hea],
        [doubled(y_rows, np.arange(-EDGE, yl + EDGE))], wx, out,
    )
    return out


def solution(mesh):
    return jax.shard_map(
        body,
        mesh=mesh,
        in_specs=(P("col", "row", None), P("col", "row", None)),
        out_specs=P("col", "row", None),
        check_vma=False,
    )
```

time: 424 us -> 111 us (0.26); the launches traced: 419 us -> 111 us
  matrix products: 153 us -> 0 us
  waiting for transfers between devices: 130 us -> 0.02 us
  Pallas kernels: 0 us -> 88.1 us
  other arithmetic: 82.7 us -> 5.44 us
  local copies, waits for them, and re-layouts: 40.2 us -> 6.5 us
    dot_general x3 -> x0, matrix products: 153 us -> none  [the longest x1 59.5 us: body(): jnp.einsum('fzyx,xw->fzyw', fields, kernel_table, precision=highest)]
    ppermute x8 -> x6, waiting for transfers between devices: 130 us -> 0.02 us  [the longest x1 0.01 us: body(): lax.ppermute(both[:, :, yl - r:, :].transpose(0, 2, 1, 3), 'row', y_up)]
    pallas_call x0 -> x3, Pallas kernels: none -> 88.1 us  [run_part(): pl.pallas_call(functools.partial(part_kernel, plan), out_shape=[jax.Shape...]
    add x1 -> x0, other arithmetic: 38.8 us -> none  [body(): return level_set + dt_step * (nu_diff * laplace + dirac_weight * forcing)]
    concatenate x1 -> x0, other arithmetic: 24.2 us -> none  [extended(): value = jnp.concatenate([before, value, after], axis=dim)]
    slice x7 -> x0, local copies, waits for them, and re-layouts: 22.3 us -> none  [the longest x2 15.1 us: body(): jnp.roll(level_set, -1, 2)]
    dot_general x1 -> x0, local copies, waits for them, and re-layouts: 16.7 us -> none  [body(): jnp.einsum('fpyx,pi->fiyx', padded_z, band_table(z_local), precision=high...]
    another operation x1 -> x7, other arithmetic: 16.4 us -> 3.53 us  [the longest x1 1.59 us: strips(): return jnp.stack([top, low])]
  transfers between devices with their start and end apart: 8 -> 6, of which waited for: 4 -> 0; matrix products, arithmetic and copies ran while one was open for 28% -> 8% of each run, Pallas kernels for 0% -> 53%
where the time goes in v2:
time: 111 us
  Pallas kernels  88.1 us (79%)
  starting transfers between devices  10.7 us (10%)
  local copies, waits for them, and re-layouts  6.5 us (6%)
  other arithmetic  5.44 us (5%)
    pallas_call x3, Pallas kernels, run_part(): pl.pallas_call(functools.partial(part_kernel, plan), out_shape=[jax.Shape...  88.1 us
    ppermute x1, starting transfers between devices, body(): lax.ppermute(both[:, :, yl - r:, :].transpose(0, 2, 1, 3), 'row', y_up)  3.07 us
    ppermute x1, starting transfers between devices, body(): corner_after = lax.ppermute(edge_first, 'col', z_down)  2.87 us
    ppermute x1, starting transfers between devices, body(): z_after = lax.ppermute(both[:, :r], 'col', z_down)  2.63 us
  transfers between devices with their start and end apart: 6, of which 0 were waited for; matrix products, arithmetic and copies ran while one was open for 8% of the time, Pallas kernels for 53%

profile of v2, /device:TPU:0, one launch (start us, length us, event | category | flops | bytes accessed | tf_op | source)
XLA Modules:
  0.0 111.1 jit_solution(10084670466147766709)
XLA Ops:
  0.0 0.0 slice-start
  0.0 0.0 slice-start.2
  0.0 1.9 %maximum_bitcast_fusion.1 = (f32[2,6,48,384]{3,1,2,0:T(8,128)S(1)}, f32[2,6,48,384]{3,1,2,0:T(8,128)S(1)}) fusion(f32[1,48,96,384]{3,2,1,0:T(8,128)} %bitcast.54, f32[1,48,96,384]{3,2,1,0:T(8,128)} %bitcast.50), kind=kLoop, calls=%fused_computation.4 | loop fusion | flops 442368 | bytes 15925248 | tf_op jit(solution)/shard_map/transpose | solution.py:381
  1.9 1.1 copy.10
  3.0 3.1 %collective-permute-start = (f32[2,6,48,384]{3,2,1,0:T(8,128)}, f32[2,6,48,384]{3,2,1,0:T(8,128)}, u32[]{:S(2)}, u32[]{:S(2)}) collective-permute-start(f32[2,6,48,384]{3,2,1,0:T(8,128)} %copy.10), channel_id=1, source_target_pairs={{0,8},{8,16},{16,24},{24,0},{1,9},{9,17},{17,25},{25,1},{2,10},{10... | collective-permute-start | bytes 2654216 | tf_op jit(solution)/shard_map/ppermute | solution.py:381
  6.1 1.1 copy.12
  7.2 2.0 %collective-permute-start.1 = (f32[2,6,48,384]{3,2,1,0:T(8,128)}, f32[2,6,48,384]{3,2,1,0:T(8,128)}, u32[]{:S(2)}, u32[]{:S(2)}) collective-permute-start(f32[2,6,48,384]{3,2,1,0:T(8,128)} %copy.12), channel_id=1, source_target_pairs={{8,0},{16,8},{24,16},{0,24},{9,1},{17,9},{25,17},{1,25},{10,2},{18... | collective-permute-start | bytes 2654216 | tf_op jit(solution)/shard_map/ppermute | solution.py:382
  9.2 0.0 slice-done
  9.2 0.0 slice-done.2
  9.2 0.0 slice-done.1
  9.2 0.0 slice-done.3
  9.3 0.2 pad_maximum_fusion.1
  9.5 0.1 collective-permute-start.4
  9.6 2.6 %collective-permute-start.5 = (f32[2,6,96,384]{3,2,1,0:T(8,128)S(1)}, f32[2,6,96,384]{3,2,1,0:T(8,128)}, u32[]{:S(2)}, u32[]{:S(2)}) collective-permute-start(f32[2,6,96,384]{3,2,1,0:T(8,128)S(1)} %get-tuple-element.11), channel_id=1, source_target_pairs={{1,0},{2,1},{3,2},{4,3},{5,4},{6,5},{7,6},{0,7},{9,8},{10,9},{11,1... | collective-permute-start | bytes 5308424 | tf_op jit(solution)/shard_map/ppermute | solution.py:384
  12.2 44.1 %interior.1 = (f32[48,96,384]{2,1,0:T(8,128)}, f32[48,96,384]{2,1,0:T(8,128)}, bf16[32,64,1536]{2,1,0:T(8,128)(2,1)}) custom-call(f32[48,96,384]{2,1,0:T(8,128)} %refs_0_.5, f32[48,96,384]{2,1,0:T(8,128)} %refs_1_.5, bf16[80,192]{1,0:T(8,128)(2,1)} %constant.30.refs_2_, bf16[768,384]{1,0:T(8,128)(2,1)} %constant.31.refs_3_.refs_6_.refs_8_), custom_call_target="tpu_custom_call" | custom-call | flops 11796480000 | bytes 11796480 | tf_op jit(solution)/shard_map/interior/pallas_call | solution.py:333
  56.4 0.0 collective-permute-done
  56.4 1.4 %copy.22 = f32[2,6,48,384]{3,1,2,0:T(8,128)S(1)} copy(f32[2,6,48,384]{3,2,1,0:T(8,128)} %collective-permute-done) | data formatting | bytes 1769472 | tf_op jit(solution)/shard_map/ppermute | solution.py:381
  57.8 0.0 collective-permute-done.1
  57.8 1.4 %copy.23 = f32[2,6,48,384]{3,1,2,0:T(8,128)S(1)} copy(f32[2,6,48,384]{3,2,1,0:T(8,128)} %collective-permute-done.1) | data formatting | bytes 1769472 | tf_op jit(solution)/shard_map/ppermute | solution.py:382
  59.3 0.8 pad_maximum_fusion.4
  60.1 0.0 collective-permute-start.2
  60.1 2.9 %collective-permute-start.3 = (f32[2,2,6,6,384]{4,2,3,1,0:T(8,128)S(1)}, f32[2,2,6,6,384]{4,2,3,1,0:T(8,128)S(1)}, u32[]{:S(2)}, u32[]{:S(2)}) collective-permute-start(f32[2,2,6,6,384]{4,2,3,1,0:T(8,128)S(1)} %pad_maximum_fusion.5), channel_id=1, source_target_pairs={{1,0},{2,1},{3,2},{4,3},{5,4},{6,5},{7,6},{0,7},{9,8},{10,9},{11,1... | collective-permute-start | bytes 663560 | tf_op jit(solution)/shard_map/ppermute | solution.py:429
  63.0 0.2 pad_bitcast_fusion
  63.3 1.6 %pad_maximum_fusion.refs_2_ = f32[2,2,48,8,384]{4,3,2,1,0:T(8,128)} fusion(f32[1,2,48,8,384]{4,3,2,1,0:T(8,128)S(1)} %get-tuple-element.27, f32[1,2,48,8,384]{4,3,2,1,0:T(8,128)S(1)} %get-tuple-element.28), kind=kLoop, calls=%fused_computation | loop fusion | flops 589824 | bytes 4718592 | tf_op jit(solution)/shard_map/stack | solution.py:434
  64.8 15.2 %y_edges.1.refs_9_ = f32[48,96,384]{2,1,0:T(8,128)} custom-call(f32[48,96,384]{2,1,0:T(8,128)} %refs_0_.5, f32[48,96,384]{2,1,0:T(8,128)} %refs_1_.5, f32[2,2,48,8,384]{4,3,2,1,0:T(8,128)} %pad_maximum_fusion.refs_2_, bf16[32,64,1536]{2,1,0:T(8,128)(2,1)} %get-tuple-element.9.refs_3_, ...), custom_call_target="tpu_custom_call", output_to_operand_aliasing={{}: (7, {})} | custom-call | flops 2359296000 | bytes 2359296 | tf_op jit(solution)/shard_map/y_edges/pallas_call | solution.py:333
  80.0 0.0 collective-permute-done.2
  80.0 1.0 slice_bitcast_fusion.5
  81.1 0.0 collective-permute-done.3
  81.2 0.9 pad_maximum_fusion.3.refs_3_
  82.1 0.0 collective-permute-done.4.refs_4_
  82.1 0.0 collective-permute-done.5.refs_5_
  82.1 28.8 %z_edges.1 = f32[48,96,384]{2,1,0:T(8,128)} custom-call(f32[48,96,384]{2,1,0:T(8,128)} %refs_0_.5, f32[48,96,384]{2,1,0:T(8,128)} %refs_1_.5, f32[2,2,48,8,384]{4,3,2,1,0:T(8,128)} %pad_maximum_fusion.refs_2_, f32[2,2,2,6,8,384]{5,4,3,2,1,0:T(8,128)} %pad_maximum_fusion.3.refs_3_, ...), custom_call_target="tpu_custom_call", output_to_operand_aliasing={{}: (9, {})} | custom-call | flops 7077888000 | bytes 7077888 | tf_op jit(solution)/shard_map/z_edges/pallas_call | solution.py:333
  (13 shorter events, 0.2 us)
Async XLA Ops:
  0.0 9.2 %slice-start = ((s8[7077888]{0:T(1024)(128)(4,1)}), s8[4194304]{0:T(1024)(128)(4,1)S(1)}, s32[]{:S(2)}) async-start(s8[7077888]{0:T(1024)(128)(4,1)} %bitcast.51), calls=%async_computation | async-start | bytes 8388608
  0.0 9.2 %slice-start.2 = ((s8[7077888]{0:T(1024)(128)(4,1)}), s8[4194304]{0:T(1024)(128)(4,1)S(1)}, s32[]{:S(2)}) async-start(s8[7077888]{0:T(1024)(128)(4,1)} %bitcast.55), calls=%async_computation.2 | async-start | bytes 8388608
  0.0 9.2 %slice-start.1 = ((s8[7077888]{0:T(1024)(128)(4,1)}), s8[2883584]{0:T(1024)(128)(4,1)S(1)}, s32[]{:S(2)}) async-start(s8[7077888]{0:T(1024)(128)(4,1)} %bitcast.51), calls=%async_computation.1 | async-start | bytes 5767168
  0.0 9.2 %slice-start.3 = ((s8[7077888]{0:T(1024)(128)(4,1)}), s8[2883584]{0:T(1024)(128)(4,1)S(1)}, s32[]{:S(2)}) async-start(s8[7077888]{0:T(1024)(128)(4,1)} %bitcast.55), calls=%async_computation.3 | async-start | bytes 5767168
  3.0 53.3 %collective-permute-start = (f32[2,6,48,384]{3,2,1,0:T(8,128)}, f32[2,6,48,384]{3,2,1,0:T(8,128)}, u32[]{:S(2)}, u32[]{:S(2)}) collective-permute-start(f32[2,6,48,384]{3,2,1,0:T(8,128)} %copy.10), channel_id=1, source_target_pairs={{0,8},{8,16},{16,24},{24,0},{1,9},{9,17},{17,25},{25,1},{2,10},{10... | collective-permute-start | bytes 2654216 | tf_op jit(solution)/shard_map/ppermute | solution.py:381
  7.2 50.6 %collective-permute-start.1 = (f32[2,6,48,384]{3,2,1,0:T(8,128)}, f32[2,6,48,384]{3,2,1,0:T(8,128)}, u32[]{:S(2)}, u32[]{:S(2)}) collective-permute-start(f32[2,6,48,384]{3,2,1,0:T(8,128)} %copy.12), channel_id=1, source_target_pairs={{8,0},{16,8},{24,16},{0,24},{9,1},{17,9},{25,17},{1,25},{10,2},{18... | collective-permute-start | bytes 2654216 | tf_op jit(solution)/shard_map/ppermute | solution.py:382
  9.5 72.6 %collective-permute-start.4 = (f32[2,6,96,384]{3,2,1,0:T(8,128)S(1)}, f32[2,6,96,384]{3,2,1,0:T(8,128)}, u32[]{:S(2)}, u32[]{:S(2)}) collective-permute-start(f32[2,6,96,384]{3,2,1,0:T(8,128)S(1)} %get-tuple-element.12), channel_id=1, source_target_pairs={{0,1},{1,2},{2,3},{3,4},{4,5},{5,6},{6,7},{7,0},{8,9},{9,10},{10,1... | collective-permute-start | bytes 5308424 | tf_op jit(solution)/shard_map/ppermute | solution.py:383
  9.6 72.5 %collective-permute-start.5 = (f32[2,6,96,384]{3,2,1,0:T(8,128)S(1)}, f32[2,6,96,384]{3,2,1,0:T(8,128)}, u32[]{:S(2)}, u32[]{:S(2)}) collective-permute-start(f32[2,6,96,384]{3,2,1,0:T(8,128)S(1)} %get-tuple-element.11), channel_id=1, source_target_pairs={{1,0},{2,1},{3,2},{4,3},{5,4},{6,5},{7,6},{0,7},{9,8},{10,9},{11,1... | collective-permute-start | bytes 5308424 | tf_op jit(solution)/shard_map/ppermute | solution.py:384
  60.1 19.9 %collective-permute-start.2 = (f32[2,2,6,6,384]{4,2,3,1,0:T(8,128)}, f32[2,2,6,6,384]{4,2,3,1,0:T(8,128)}, u32[]{:S(2)}, u32[]{:S(2)}) collective-permute-start(f32[2,2,6,6,384]{4,2,3,1,0:T(8,128)} %pad_maximum_fusion.4), channel_id=1, source_target_pairs={{0,1},{1,2},{2,3},{3,4},{4,5},{5,6},{6,7},{7,0},{8,9},{9,10},{10,1... | collective-permute-start | bytes 663560 | tf_op jit(solution)/shard_map/ppermute | solution.py:428
  60.1 21.0 %collective-permute-start.3 = (f32[2,2,6,6,384]{4,2,3,1,0:T(8,128)S(1)}, f32[2,2,6,6,384]{4,2,3,1,0:T(8,128)S(1)}, u32[]{:S(2)}, u32[]{:S(2)}) collective-permute-start(f32[2,2,6,6,384]{4,2,3,1,0:T(8,128)S(1)} %pad_maximum_fusion.5), channel_id=1, source_target_pairs={{1,0},{2,1},{3,2},{4,3},{5,4},{6,5},{7,6},{0,7},{9,8},{10,9},{11,1... | collective-permute-start | bytes 663560 | tf_op jit(solution)/shard_map/ppermute | solution.py:429
